TPU v7x, 32 devices: a whole 2x2x4 slice. The times are simulated.
32 devices in a mesh: strip: 8 (over z, x), col: 4 (over y, core).
Axes of the slice: x: 2, y: 2, z: 4, core: 2. Of those that a mesh axis runs over, the one named last changes fastest.
Arguments:
- net_box: int32 [32768, 4], P(('strip', 'col')), may hold values from 0 to 1023, as said below
- net_weight: float32 [32768], P(('strip', 'col')), may hold values from 0.5 to 2
- pin_bin: int32 [32768, 4, 2], P(('strip', 'col')), may hold values from 0 to 1023, as said below
- conv_first: bfloat16 [3, 3, 32, 3], replicated, may hold values from -1.25 to 1.25
- bias_first: float32 [32], replicated, may hold values from -3 to 3
- conv_second: bfloat16 [3, 3, 32, 32], replicated, may hold values from -0.375 to 0.375
- bias_second: float32 [32], replicated, may hold values from -3 to 3
- cotangent: bfloat16 [512, 32, 1024], P('col', None, 'strip'), may hold values from -6 to 6
Outputs:
- congestion: bfloat16 [512, 32, 1024], P('col', None, 'strip')
- net_grad: float32 [32768], P(('strip', 'col'))
Inputs may be any that keep to these rules, and one draw needn't show every extreme that they name: `net_box`: box n = (x0, x1, y0, y1) has x0 <= x1 < x0 + 16 and y0 <= y1 < y0 + 16; y0 lies in rows s * 128 to (s + 1) * 128 - 1, where s = n // 4096 is the strip whose devices hold net n. Some box is 16 bins tall and wide. `pin_bin`: every pin of net n lies in net n's box.
All inputs are finite; a program needn't handle non-finite values.
Results may differ from a plain program's by a relative error of at most 0.0054.
Values may be sent and summed in bfloat16 or wider, within the bound.
No kernel may reach another device: no remote copies, remote signals or barrier semaphores. Data moves between devices by JAX's collectives and lax.ppermute only.
A program may use at most 192 MiB of HBM per device.

v0:
```python
import math
import jax
import jax.numpy as jnp
from jax import lax
from jax.sharding import PartitionSpec as P


def from_behind(x, axis, by):
    size = lax.axis_size(axis)
    pairs = [(i, i + by) for i in range(size) if 0 <= i + by < size]
    return lax.ppermute(x, axis, pairs)


def with_halo(block, sides, width):
    for axis, dim in sides:
        count = lax.axis_size(axis)
        forward = [(i, i + 1) for i in range(count - 1)]
        backward = [(target, source) for source, target in forward]
        low = lax.ppermute(
            lax.slice_in_dim(block, block.shape[dim] - width, None, axis=dim), axis, forward
        )
        high = lax.ppermute(lax.slice_in_dim(block, 0, width, axis=dim), axis, backward)
        block = jnp.concatenate([low, block, high], axis=dim)
    return block


def silu_slope(pre_act):
    sigmoid = jax.nn.sigmoid(pre_act)
    return sigmoid * (1.0 + pre_act * (1.0 - sigmoid))


def conv_valid(padded, weights, out_cols, out_rows):
    summed = None
    for shift_row in range(3):
        for shift_col in range(3):
            window = padded[shift_col : shift_col + out_cols, :, shift_row : shift_row + out_rows]
            product = jnp.einsum(
                "oi,xiy->xoy",
                weights[shift_row, shift_col],
                window,
                preferred_element_type=jnp.float32,
            )
            summed = product if summed is None else summed + product
    return summed


def conv_back(padded, weights, out_cols, out_rows):
    summed = None
    for shift_row in range(3):
        for shift_col in range(3):
            window = padded[
                2 - shift_col : 2 - shift_col + out_cols,
                :,
                2 - shift_row : 2 - shift_row + out_rows,
            ]
            product = jnp.einsum(
                "oi,xoy->xiy",
                weights[shift_row, shift_col],
                window,
                preferred_element_type=jnp.float32,
            )
            summed = product if summed is None else summed + product
    return summed


def strip_factors(box_rows, weights, pin_list, first_row, span):
    row_ids = first_row + jnp.arange(2 * span, dtype=jnp.int32)
    top_row = box_rows[:, 2]
    bottom_row = box_rows[:, 3]
    inside = (top_row[:, None] <= row_ids[None, :]) & (row_ids[None, :] <= bottom_row[:, None])
    box_height = (bottom_row - top_row + 1).astype(jnp.float32)
    box_width = (box_rows[:, 1] - box_rows[:, 0] + 1).astype(jnp.float32)
    values = jnp.stack([weights / box_height, weights / box_width], axis=1).astype(jnp.bfloat16)
    row_factor = inside.astype(jnp.bfloat16).reshape(-1, 2, 1, span) * values[:, None, :, None]
    pin_rows = pin_list[:, :, 0].reshape(-1)
    pin_factor = (pin_rows[:, None] == row_ids[None, :]).astype(jnp.bfloat16).reshape(-1, 2, span)
    return (row_factor, pin_list[:, :, 1].reshape(-1), pin_factor)


def column_block(col_ids, left_col, right_col, row_factor, pin_col, pin_factor):
    net_cols = (
        (left_col[:, None] <= col_ids[None, :]) & (col_ids[None, :] <= right_col[:, None])
    ).astype(jnp.bfloat16)
    pin_cols = (pin_col[:, None] == col_ids[None, :]).astype(jnp.bfloat16)
    demand = jnp.einsum("nk,nhcr->khcr", net_cols, row_factor, preferred_element_type=jnp.float32)
    density = jnp.einsum("pk,phr->khr", pin_cols, pin_factor, preferred_element_type=jnp.float32)
    return jnp.concatenate([demand, density[:, :, None, :]], axis=2)


def shards(
    net_box, net_weight, pin_bin, conv_first, bias_first, conv_second, bias_second, cotangent
):
    tile_cols = cotangent.shape[0]
    span = cotangent.shape[2]
    net_total = net_box.shape[0]
    strip_index = lax.axis_index("strip")
    col_index = lax.axis_index("col")
    all_rows = span * lax.axis_size("strip")
    all_cols = tile_cols * lax.axis_size("col")
    first_row = strip_index * span
    pin_width = pin_bin.shape[1]
    packed = jnp.concatenate(
        [
            net_box.astype(jnp.float32),
            pin_bin.reshape(net_total, 2 * pin_width).astype(jnp.float32),
            net_weight[:, None],
        ],
        axis=1,
    )
    own_cols = col_index * tile_cols + jnp.arange(tile_cols, dtype=jnp.int32)
    start_terms = jnp.zeros((tile_cols, 2, 3, span), jnp.float32)
    shard_piece = lax.all_gather(packed, "col", axis=0, tiled=True)
    piece_rows = shard_piece.shape[0]
    block_size = math.gcd(piece_rows, 1024)
    grouped = shard_piece.reshape(piece_rows // block_size, block_size, shard_piece.shape[1])

    def one_group(summed, net_group):
        box_rows = net_group[:, :4].astype(jnp.int32)
        pin_list = (
            net_group[:, 4 : 4 + 2 * pin_width].reshape(block_size, pin_width, 2).astype(jnp.int32)
        )
        weights = net_group[:, 4 + 2 * pin_width]
        row_factor, pin_col, pin_factor = strip_factors(
            box_rows, weights, pin_list, first_row, span
        )
        return (
            summed
            + column_block(
                own_cols, box_rows[:, 0], box_rows[:, 1], row_factor, pin_col, pin_factor
            ),
            None,
        )

    summed, unused = lax.scan(one_group, start_terms, grouped)
    spilled = from_behind(summed[:, 1].astype(jnp.bfloat16), "strip", 1).astype(jnp.float32)
    features = (summed[:, 0] + spilled).astype(jnp.bfloat16)
    stacked = jnp.concatenate([features, cotangent], axis=1)
    padded = with_halo(stacked, (("strip", 2), ("col", 0)), 2)
    in_channels = features.shape[1]
    col_ids = col_index * tile_cols - 1 + jnp.arange(tile_cols + 2, dtype=jnp.int32)
    row_ids = first_row - 1 + jnp.arange(span + 2, dtype=jnp.int32)
    inside = ((col_ids >= 0) & (col_ids < all_cols))[:, None, None] & (
        (row_ids >= 0) & (row_ids < all_rows)
    )[None, None, :]
    pre_act = (
        conv_valid(padded[:, :in_channels], conv_first, tile_cols + 2, span + 2)
        + bias_first[None, :, None]
    )
    hidden = jnp.where(inside, jax.nn.silu(pre_act), 0.0).astype(jnp.bfloat16)
    congestion = (
        conv_valid(hidden, conv_second, tile_cols, span) + bias_second[None, :, None]
    ).astype(jnp.bfloat16)
    back_hidden = conv_back(padded[:, in_channels:], conv_second, tile_cols + 2, span + 2)
    back_pre = jnp.where(inside, back_hidden * silu_slope(pre_act), 0.0).astype(jnp.bfloat16)
    back_maps = conv_back(back_pre, conv_first[:, :, :, :2], tile_cols, span).astype(jnp.bfloat16)
    from_below = from_behind(back_maps, "strip", -1)
    both_halves = jnp.stack([back_maps, from_below], axis=1).reshape(tile_cols, 4 * span)
    left_col = net_box[:, 0]
    right_col = net_box[:, 1]
    shard_piece = lax.all_gather(both_halves, "col", axis=0, tiled=True)
    piece_cols = jnp.arange(shard_piece.shape[0], dtype=jnp.int32)
    net_cols = (
        (left_col[:, None] <= piece_cols[None, :]) & (piece_cols[None, :] <= right_col[:, None])
    ).astype(jnp.bfloat16)
    column_sums = jnp.dot(net_cols, shard_piece, preferred_element_type=jnp.float32)
    column_sums = column_sums.reshape(net_total, 2, 2, span)
    net_rows = first_row + jnp.arange(2 * span, dtype=jnp.int32)
    in_rows = (
        (
            (net_box[:, 2][:, None] <= net_rows[None, :])
            & (net_rows[None, :] <= net_box[:, 3][:, None])
        )
        .astype(jnp.float32)
        .reshape(net_total, 2, span)
    )
    box_height = (net_box[:, 3] - net_box[:, 2] + 1).astype(jnp.float32)
    box_width = (right_col - left_col + 1).astype(jnp.float32)
    per_row = (
        column_sums[:, :, 0] / box_height[:, None, None]
        + column_sums[:, :, 1] / box_width[:, None, None]
    )
    net_grad = jnp.sum(in_rows * per_row, axis=(1, 2))
    return (congestion, net_grad)


def solution(mesh):
    placed = (
        P(("strip", "col"), None),
        P(("strip", "col")),
        P(("strip", "col"), None, None),
        P(),
        P(),
        P(),
        P(),
        P("col", None, "strip"),
    )
    return jax.shard_map(
        shards,
        mesh=mesh,
        in_specs=placed,
        out_specs=(P("col", None, "strip"), P(("strip", "col"))),
        check_vma=False,
    )
```

profile of v0, /device:TPU:19, one launch (start us, length us, event | category | flops | bytes accessed | tf_op | source)
XLA Modules:
  0.0 179.9 jit_solution(665664036078959381)
XLA Ops:
  0.6 0.8 convert_element_type.81
  1.5 0.7 convert_element_type.80
  2.2 0.7 pad_maximum_fusion.10
  2.9 6.3 %all_gather.6 = f32[4096,13]{0,1:T(8,128)S(1)} all-gather(f32[1024,13]{0,1:T(8,128)S(1)} %pad_maximum_fusion.10), channel_id=1, replica_groups=mesh['strip'=8,'col'=4] {'col'}, dimensions={0}, use_global_device_ids=true | all-gather | bytes 266240 | tf_op jit(solution)/shard_map/all_gather | solution.py:112
  9.4 13.7 %while.11 = (s32[]{:T(128)}, f32[128,2,3,128]{3,0,2,1:T(8,128)S(1)}, f32[4,1024,13]{1,0,2:T(4,128)S(1)}, s32[]{:T(128)}, s32[]{:T(128)}, /*index=5*/s32[]{:T(128)}, s32[]{:T(128)}) while((s32[]{:T(128)}, f32[128,2,3,128]{3,0,2,1:T(8,128)S(1)}, f32[4,1024,13]{1,0,2:T(4,128)S(1)}, s32[]{:T(128)}, s32[]{:T(128)}, ...), condition=%wide.region_1.2_spmd.clone, body=%wide.region_0.1_spmd.clone.sunk | while | flops 408091520 | bytes 3318379 | solution.py:134
  10.6 1.1 fusion.251
  12.1 0.5 fusion.254
  14.0 1.1 fusion.251
  15.5 0.5 fusion.254
  17.4 1.1 fusion.251
  19.0 0.5 fusion.254
  20.9 1.1 fusion.251
  22.4 0.5 fusion.254
  23.3 3.2 %collective-permute-start = (bf16[128,3,128]{0,2,1:T(8,128)(2,1)S(1)}, bf16[128,3,128]{0,2,1:T(8,128)(2,1)S(1)}, u32[]{:S(2)}, u32[]{:S(2)}) collective-permute-start(bf16[128,3,128]{0,2,1:T(8,128)(2,1)S(1)} %fusion.144), channel_id=1, source_target_pairs={{0,4},{4,8},{8,12},{12,16},{16,20},{20,24},{24,28},{1,5},{5,9},{9,... | collective-permute-start | bytes 294920 | tf_op jit(solution)/shard_map/ppermute | solution.py:11
  26.6 1.0 copy.57
  27.6 1.8 %collective-permute-done = bf16[128,3,128]{0,2,1:T(8,128)(2,1)S(1)} collective-permute-done((bf16[128,3,128]{0,2,1:T(8,128)(2,1)S(1)}, bf16[128,3,128]{0,2,1:T(8,128)(2,1)S(1)}, u32[]{:S(2)}, u32[]{:S(2)}) %collective-permute-start) | collective-permute-done | bytes 98336 | tf_op jit(solution)/shard_map/ppermute | solution.py:11
  29.5 3.1 %collective-permute-start.2 = (bf16[128,35,2]{0,2,1:T(2,128)(2,1)S(1)}, bf16[128,35,2]{0,2,1:T(2,128)(2,1)S(1)}, u32[]{:S(2)}, u32[]{:S(2)}) collective-permute-start(bf16[128,35,2]{0,2,1:T(2,128)(2,1)S(1)} %get-tuple-element.87), channel_id=1, source_target_pairs={{4,0},{8,4},{12,8},{16,12},{20,16},{24,20},{28,24},{5,1},{9,5},{13... | collective-permute-start | bytes 53768 | tf_op jit(solution)/shard_map/ppermute | solution.py:22
  32.6 3.1 %collective-permute-start.1 = (bf16[128,35,2]{0,2,1:T(2,128)(2,1)S(1)}, bf16[128,35,2]{0,2,1:T(2,128)(2,1)S(1)}, u32[]{:S(2)}, u32[]{:S(2)}) collective-permute-start(bf16[128,35,2]{0,2,1:T(2,128)(2,1)S(1)} %get-tuple-element.86), channel_id=1, source_target_pairs={{0,4},{4,8},{8,12},{12,16},{16,20},{20,24},{24,28},{1,5},{5,9},{9,... | collective-permute-start | bytes 53768 | tf_op jit(solution)/shard_map/ppermute | solution.py:19
  35.7 1.3 collective-permute-done.1
  37.1 1.6 pad_maximum_fusion.8
  38.7 3.6 %copy.58 = bf16[128,35,132]{2,1,0:T(8,128)(2,1)S(1)} copy(bf16[128,35,132]{0,2,1:T(8,128)(2,1)} %pad_maximum_fusion.8) | data formatting | bytes 2365440 | tf_op jit(solution)/shard_map/concatenate | solution.py:23
  42.3 5.4 %collective-permute-start.3 = (bf16[2,35,132]{2,1,0:T(8,128)(2,1)S(1)}, bf16[2,35,132]{2,1,0:T(8,128)(2,1)S(1)}, u32[]{:S(2)}, u32[]{:S(2)}) collective-permute-start(bf16[2,35,132]{2,1,0:T(8,128)(2,1)S(1)} %get-tuple-element.84), channel_id=1, source_target_pairs={{0,1},{1,2},{2,3},{4,5},{5,6},{6,7},{8,9},{9,10},{10,11},{12,13},{... | collective-permute-start | bytes 55448 | tf_op jit(solution)/shard_map/ppermute | solution.py:19
  47.8 2.1 %collective-permute-start.4 = (bf16[2,35,132]{2,1,0:T(8,128)(2,1)S(1)}, bf16[2,35,132]{2,1,0:T(8,128)(2,1)S(1)}, u32[]{:S(2)}, u32[]{:S(2)}) collective-permute-start(bf16[2,35,132]{2,1,0:T(8,128)(2,1)S(1)} %get-tuple-element.85), channel_id=1, source_target_pairs={{1,0},{2,1},{3,2},{5,4},{6,5},{7,6},{9,8},{10,9},{11,10},{13,12},{... | collective-permute-start | bytes 55448 | tf_op jit(solution)/shard_map/ppermute | solution.py:22
  49.9 2.7 %fusion.110 = f32[130,130,32]{1,2,0:T(8,128)} fusion(bf16[128,35,132]{2,1,0:T(8,128)(2,1)S(1)} %copy.58, bf16[2,35,132]{2,1,0:T(8,128)(2,1)S(1)} %collective-permute-done.3, bf16[3,3,32,3]{2,3,1,0:T(4,128)(2,1)S(1)} %copy-done.10), kind=kOutput, calls=%fused_computation.139 | convolution fusion | flops 3447600 | bytes 4826624 | tf_op jit(solution)/shard_map/oi,xiy->xoy/dot_general | solution.py:37
  53.1 2.9 %fusion.104 = f32[130,130,32]{1,2,0:T(8,128)} fusion(bf16[2,35,132]{2,1,0:T(8,128)(2,1)S(1)} %collective-permute-done.4, bf16[128,35,132]{2,1,0:T(8,128)(2,1)S(1)} %copy.58, bf16[2,35,132]{2,1,0:T(8,128)(2,1)S(1)} %collective-permute-done.3, bf16[3,3,32,3]{2,3,1,0:T(4,128)(2,1)S(1)} %copy-done.10), kind=kOutput, calls=%fused_computation.133 | convolution fusion | flops 3549000 | bytes 4867584 | tf_op jit(solution)/shard_map/oi,xiy->xoy/dot_general | solution.py:37
  56.0 2.8 %fusion.114 = f32[130,130,32]{1,2,0:T(8,128)} fusion(bf16[2,35,132]{2,1,0:T(8,128)(2,1)S(1)} %collective-permute-done.4, bf16[128,35,132]{2,1,0:T(8,128)(2,1)S(1)} %copy.58, bf16[3,3,32,3]{2,3,1,0:T(4,128)(2,1)S(1)} %copy-done.10), kind=kOutput, calls=%fused_computation.143 | convolution fusion | flops 3447600 | bytes 4826624 | tf_op jit(solution)/shard_map/oi,xiy->xoy/dot_general | solution.py:37
  58.8 2.8 %fusion.118 = f32[130,130,32]{1,2,0:T(8,128)} fusion(bf16[2,35,132]{2,1,0:T(8,128)(2,1)S(1)} %collective-permute-done.4, bf16[128,35,132]{2,1,0:T(8,128)(2,1)S(1)} %copy.58, bf16[2,35,132]{2,1,0:T(8,128)(2,1)S(1)} %collective-permute-done.3, bf16[3,3,32,3]{2,3,1,0:T(4,128)(2,1)S(1)} %copy-done.10), kind=kOutput, calls=%fused_computation.147 | convolution fusion | flops 3549000 | bytes 4867584 | tf_op jit(solution)/shard_map/oi,xiy->xoy/dot_general | solution.py:37
  61.6 2.7 %fusion.124 = f32[130,130,32]{1,2,0:T(8,128)} fusion(bf16[128,35,132]{2,1,0:T(8,128)(2,1)S(1)} %copy.58, bf16[2,35,132]{2,1,0:T(8,128)(2,1)S(1)} %collective-permute-done.3, bf16[3,3,32,3]{2,3,1,0:T(4,128)(2,1)S(1)} %copy-done.10), kind=kOutput, calls=%fused_computation.153 | convolution fusion | flops 3447600 | bytes 4826624 | tf_op jit(solution)/shard_map/oi,xiy->xoy/dot_general | solution.py:37
  64.3 2.7 %fusion.128 = f32[130,130,32]{1,2,0:T(8,128)} fusion(bf16[2,35,132]{2,1,0:T(8,128)(2,1)S(1)} %collective-permute-done.4, bf16[128,35,132]{2,1,0:T(8,128)(2,1)S(1)} %copy.58, bf16[3,3,32,3]{2,3,1,0:T(4,128)(2,1)S(1)} %copy-done.10), kind=kOutput, calls=%fused_computation.157 | convolution fusion | flops 3447600 | bytes 4826624 | tf_op jit(solution)/shard_map/oi,xiy->xoy/dot_general | solution.py:37
  67.0 2.8 %fusion.138 = f32[130,130,32]{1,2,0:T(8,128)} fusion(bf16[128,35,132]{2,1,0:T(8,128)(2,1)S(1)} %copy.58, bf16[2,35,132]{2,1,0:T(8,128)(2,1)S(1)} %collective-permute-done.3, bf16[3,3,32,3]{2,3,1,0:T(4,128)(2,1)S(1)} %copy-done.10), kind=kOutput, calls=%fused_computation.167 | convolution fusion | flops 3447600 | bytes 4826624 | tf_op jit(solution)/shard_map/oi,xiy->xoy/dot_general | solution.py:37
  69.8 2.8 %fusion.132 = f32[130,130,32]{1,2,0:T(8,128)} fusion(bf16[2,35,132]{2,1,0:T(8,128)(2,1)S(1)} %collective-permute-done.4, bf16[128,35,132]{2,1,0:T(8,128)(2,1)S(1)} %copy.58, bf16[2,35,132]{2,1,0:T(8,128)(2,1)S(1)} %collective-permute-done.3, bf16[3,3,32,3]{2,3,1,0:T(4,128)(2,1)S(1)} %copy-done.10), kind=kOutput, calls=%fused_computation.161 | convolution fusion | flops 3549000 | bytes 4867584 | tf_op jit(solution)/shard_map/oi,xiy->xoy/dot_general | solution.py:37
  72.6 14.8 %fusion.34 = (bf16[130,32,130]{2,1,0:T(8,128)(2,1)S(1)}, f32[130,130,32]{1,2,0:T(8,128)}) fusion(pred[130,130]{1,0:T(8,128)(4,1)S(1)} %broadcast_and_fusion, f32[32]{0:T(128)S(1)} %copy-done.12, bf16[3,3,32,3]{2,3,1,0:T(4,128)(2,1)S(1)} %copy-done.10, bf16[2,35,132]{2,1,0:T(8,128)(2,1)S(1)} %collective-permute-done.4, bf16[128,35,132]{2,1,0:T(8,128)(2,1)S(1)} %copy.58, ...), kind=kOutput, calls=%fused_computation.44 | convolution fusion | flops 11559600 | bytes 23249152 | tf_op jit(solution)/shard_map/oi,xiy->xoy/dot_general | solution.py:37
  87.5 1.9 %fusion.79 = f32[128,128,32]{1,2,0:T(8,128)} fusion(bf16[130,32,130]{2,1,0:T(8,128)(2,1)S(1)} %get-tuple-element.92, bf16[3,3,32,32]{3,2,1,0:T(8,128)(2,1)S(1)} %copy-done.8), kind=kOutput, calls=%fused_computation.110 | convolution fusion | flops 33554432 | bytes 3153920 | tf_op jit(solution)/shard_map/oi,xiy->xoy/dot_general | solution.py:37
  89.4 1.9 %fusion.81 = f32[128,128,32]{1,2,0:T(8,128)} fusion(bf16[130,32,130]{2,1,0:T(8,128)(2,1)S(1)} %get-tuple-element.92, bf16[3,3,32,32]{3,2,1,0:T(8,128)(2,1)S(1)} %copy-done.8), kind=kOutput, calls=%fused_computation.112 | convolution fusion | flops 33554432 | bytes 3153920 | tf_op jit(solution)/shard_map/oi,xiy->xoy/dot_general | solution.py:37
  91.2 1.9 %fusion.83 = f32[128,128,32]{1,2,0:T(8,128)} fusion(bf16[130,32,130]{2,1,0:T(8,128)(2,1)S(1)} %get-tuple-element.92, bf16[3,3,32,32]{3,2,1,0:T(8,128)(2,1)S(1)} %copy-done.8), kind=kOutput, calls=%fused_computation.114 | convolution fusion | flops 33554432 | bytes 3153920 | tf_op jit(solution)/shard_map/oi,xiy->xoy/dot_general | solution.py:37
  93.1 1.8 %fusion.85 = f32[128,128,32]{1,2,0:T(8,128)} fusion(bf16[130,32,130]{2,1,0:T(8,128)(2,1)S(1)} %get-tuple-element.92, bf16[3,3,32,32]{3,2,1,0:T(8,128)(2,1)S(1)} %copy-done.8), kind=kOutput, calls=%fused_computation.116 | convolution fusion | flops 33554432 | bytes 3153920 | tf_op jit(solution)/shard_map/oi,xiy->xoy/dot_general | solution.py:37
  95.0 1.8 %fusion.87 = f32[128,128,32]{1,2,0:T(8,128)} fusion(bf16[130,32,130]{2,1,0:T(8,128)(2,1)S(1)} %get-tuple-element.92, bf16[3,3,32,32]{3,2,1,0:T(8,128)(2,1)S(1)} %copy-done.8), kind=kOutput, calls=%fused_computation.118 | convolution fusion | flops 33554432 | bytes 3153920 | tf_op jit(solution)/shard_map/oi,xiy->xoy/dot_general | solution.py:37
  96.8 1.8 fusion.89
  98.6 1.7 fusion.93
  100.3 1.7 fusion.91
  102.0 0.6 pad_maximum_fusion.1
  102.6 2.7 %fusion.51 = f32[130,130,32]{1,2,0:T(8,128)} fusion(bf16[132,35,132]{2,1,0:T(8,128)(2,1)S(1)} %pad_maximum_fusion.1, bf16[3,3,32,32]{3,2,1,0:T(8,128)(2,1)S(1)} %copy-done.8), kind=kOutput, calls=%fused_computation.68 | convolution fusion | flops 34611200 | bytes 4301312 | tf_op jit(solution)/shard_map/oi,xoy->xiy/dot_general | solution.py:56
  105.3 3.1 %fusion.55 = f32[130,130,32]{1,2,0:T(8,128)} fusion(bf16[132,35,132]{2,1,0:T(8,128)(2,1)S(1)} %pad_maximum_fusion.1, bf16[3,3,32,32]{3,2,1,0:T(8,128)(2,1)S(1)} %copy-done.8), kind=kOutput, calls=%fused_computation.73 | convolution fusion | flops 34611200 | bytes 4301312 | tf_op jit(solution)/shard_map/oi,xoy->xiy/dot_general | solution.py:56
  108.5 3.2 %fusion.57 = f32[130,130,32]{1,2,0:T(8,128)} fusion(bf16[132,35,132]{2,1,0:T(8,128)(2,1)S(1)} %pad_maximum_fusion.1, bf16[3,3,32,32]{3,2,1,0:T(8,128)(2,1)S(1)} %copy-done.8), kind=kOutput, calls=%fused_computation.75 | convolution fusion | flops 34611200 | bytes 4301312 | tf_op jit(solution)/shard_map/oi,xoy->xiy/dot_general | solution.py:56
  111.6 2.8 %fusion.53 = f32[130,130,32]{1,2,0:T(8,128)} fusion(bf16[2,35,132]{2,1,0:T(8,128)(2,1)S(1)} %collective-permute-done.4, bf16[128,35,132]{2,1,0:T(8,128)(2,1)S(1)} %copy.58, bf16[3,3,32,32]{3,2,1,0:T(8,128)(2,1)S(1)} %copy-done.8), kind=kOutput, calls=%fused_computation.71 | convolution fusion | flops 36774400 | bytes 4833792 | tf_op jit(solution)/shard_map/oi,xoy->xiy/dot_general | solution.py:56
  114.5 3.6 %fusion.44 = f32[130,130,32]{1,2,0:T(8,128)} fusion(bf16[128,35,132]{2,1,0:T(8,128)(2,1)S(1)} %copy.58, bf16[2,35,132]{2,1,0:T(8,128)(2,1)S(1)} %collective-permute-done.3, bf16[3,3,32,32]{3,2,1,0:T(8,128)(2,1)S(1)} %copy-done.8), kind=kOutput, calls=%fused_computation.62 | convolution fusion | flops 35152000 | bytes 4833792 | tf_op jit(solution)/shard_map/oi,xoy->xiy/dot_general | solution.py:56
  118.1 3.6 %fusion.38 = f32[130,130,32]{1,2,0:T(8,128)} fusion(bf16[128,35,132]{2,1,0:T(8,128)(2,1)S(1)} %copy.58, bf16[2,35,132]{2,1,0:T(8,128)(2,1)S(1)} %collective-permute-done.4, bf16[3,3,32,32]{3,2,1,0:T(8,128)(2,1)S(1)} %copy-done.8), kind=kOutput, calls=%fused_computation.58 | convolution fusion | flops 35152000 | bytes 4833792 | tf_op jit(solution)/shard_map/oi,xoy->xiy/dot_general | solution.py:56
  121.7 3.9 %fusion.47 = f32[130,130,32]{1,2,0:T(8,128)} fusion(bf16[128,35,132]{2,1,0:T(8,128)(2,1)S(1)} %copy.58, bf16[2,35,132]{2,1,0:T(8,128)(2,1)S(1)} %collective-permute-done.3, bf16[3,3,32,32]{3,2,1,0:T(8,128)(2,1)S(1)} %copy-done.8), kind=kOutput, calls=%fused_computation.64 | convolution fusion | flops 35152000 | bytes 4833792 | tf_op jit(solution)/shard_map/oi,xoy->xiy/dot_general | solution.py:56
  125.7 3.7 %fusion.41 = f32[130,130,32]{1,2,0:T(8,128)} fusion(bf16[128,35,132]{2,1,0:T(8,128)(2,1)S(1)} %copy.58, bf16[2,35,132]{2,1,0:T(8,128)(2,1)S(1)} %collective-permute-done.4, bf16[3,3,32,32]{3,2,1,0:T(8,128)(2,1)S(1)} %copy-done.8), kind=kOutput, calls=%fused_computation.60 | convolution fusion | flops 35152000 | bytes 4833792 | tf_op jit(solution)/shard_map/oi,xoy->xiy/dot_general | solution.py:56
  129.4 15.3 %fusion.29 = bf16[130,32,130]{2,1,0:T(8,128)(2,1)} fusion(f32[130,130,32]{1,2,0:T(8,128)} %get-tuple-element.93, f32[130,130,32]{1,2,0:T(8,128)} %fusion.51, f32[130,130,32]{1,2,0:T(8,128)} %fusion.53, f32[130,130,32]{1,2,0:T(8,128)} %fusion.44, f32[130,130,32]{1,2,0:T(8,128)} %fusion.55, f32[130,130,32]{1,2,0:T(8,128)} %fusion.38, ...), kind=kOutput, calls=%fused_computation.36 | convolution fusion | flops 46508800 | bytes 23255808 | tf_op jit(solution)/shard_map/oi,xoy->xiy/dot_general | solution.py:56
  144.7 2.1 %fusion.76 = f32[128,128,2]{1,2,0:T(2,128)S(1)} fusion(bf16[130,32,130]{2,1,0:T(8,128)(2,1)} %fusion.29, bf16[3,3,32,3]{2,3,1,0:T(4,128)(2,1)S(1)} %copy-done.10), kind=kOutput, calls=%fused_computation.107 | convolution fusion | flops 2097152 | bytes 1180160 | tf_op jit(solution)/shard_map/oi,xoy->xiy/dot_general | solution.py:56
  146.8 2.2 %convolution_add_fusion.7 = f32[128,128,2]{1,2,0:T(2,128)S(1)} fusion(f32[128,128,2]{1,2,0:T(2,128)S(1)} %fusion.76, bf16[130,32,130]{2,1,0:T(8,128)(2,1)} %fusion.29, bf16[3,3,32,3]{2,3,1,0:T(4,128)(2,1)S(1)} %copy-done.10), kind=kOutput, calls=%fused_computation.91 | convolution fusion | flops 2129920 | bytes 1311232 | tf_op jit(solution)/shard_map/oi,xoy->xiy/dot_general | solution.py:56
  149.0 2.2 %convolution_add_fusion.6 = f32[128,128,2]{1,2,0:T(2,128)S(1)} fusion(f32[128,128,2]{1,2,0:T(2,128)S(1)} %convolution_add_fusion.7, bf16[130,32,130]{2,1,0:T(8,128)(2,1)} %fusion.29, bf16[3,3,32,3]{2,3,1,0:T(4,128)(2,1)S(1)} %copy-done.10), kind=kOutput, calls=%fused_computation.90 | convolution fusion | flops 2129920 | bytes 1311232 | tf_op jit(solution)/shard_map/oi,xoy->xiy/dot_general | solution.py:56
  151.3 2.1 %convolution_add_fusion.5 = f32[128,128,2]{1,2,0:T(2,128)S(1)} fusion(f32[128,128,2]{1,2,0:T(2,128)S(1)} %convolution_add_fusion.6, bf16[130,32,130]{2,1,0:T(8,128)(2,1)} %fusion.29, bf16[3,3,32,3]{2,3,1,0:T(4,128)(2,1)S(1)} %copy-done.10), kind=kOutput, calls=%fused_computation.89 | convolution fusion | flops 2129920 | bytes 1311232 | tf_op jit(solution)/shard_map/oi,xoy->xiy/dot_general | solution.py:56
  153.4 2.2 %convolution_add_fusion.4 = f32[128,128,2]{1,2,0:T(2,128)S(1)} fusion(f32[128,128,2]{1,2,0:T(2,128)S(1)} %convolution_add_fusion.5, bf16[130,32,130]{2,1,0:T(8,128)(2,1)} %fusion.29, bf16[3,3,32,3]{2,3,1,0:T(4,128)(2,1)S(1)} %copy-done.10), kind=kOutput, calls=%fused_computation.88 | convolution fusion | flops 2129920 | bytes 1311232 | tf_op jit(solution)/shard_map/oi,xoy->xiy/dot_general | solution.py:56
  155.6 2.2 %convolution_add_fusion.3 = f32[128,128,2]{1,2,0:T(2,128)S(1)} fusion(f32[128,128,2]{1,2,0:T(2,128)S(1)} %convolution_add_fusion.4, bf16[130,32,130]{2,1,0:T(8,128)(2,1)} %fusion.29, bf16[3,3,32,3]{2,3,1,0:T(4,128)(2,1)S(1)} %copy-done.10), kind=kOutput, calls=%fused_computation.87 | convolution fusion | flops 2129920 | bytes 1311232 | tf_op jit(solution)/shard_map/oi,xoy->xiy/dot_general | solution.py:56
  157.9 1.5 convolution_add_fusion.2
  159.4 1.5 convolution_add_fusion.1
  160.8 1.5 fusion.63
  162.3 3.0 %collective-permute-start.5 = (bf16[128,2,128]{2,1,0:T(2,128)(2,1)S(1)}, bf16[128,2,128]{2,1,0:T(2,128)(2,1)S(1)}, u32[]{:S(2)}, u32[]{:S(2)}) collective-permute-start(bf16[128,2,128]{2,1,0:T(2,128)(2,1)S(1)} %bitcast.290), channel_id=1, source_target_pairs={{4,0},{8,4},{12,8},{16,12},{20,16},{24,20},{28,24},{5,1},{9,5},{13... | collective-permute-start | bytes 196616 | tf_op jit(solution)/shard_map/ppermute | solution.py:11
  165.4 4.2 %fusion.62 = bf16[128,32,128]{2,1,0:T(8,128)(2,1)} fusion(f32[128,128,32]{1,2,0:T(8,128)S(1)} %copy-done, f32[128,128,32]{1,2,0:T(8,128)S(1)} %copy-done.1, f32[128,128,32]{1,2,0:T(8,128)S(1)} %copy-done.2, f32[128,128,32]{1,2,0:T(8,128)S(1)} %copy-done.3, f32[128,128,32]{1,2,0:T(8,128)S(1)} %copy-done.4, f32[128,128,32]{1,2,0:T(8,128)S(1)} %copy-done.5, ...), kind=kOutput, calls=%fused_computation.82 | convolution fusion | flops 38797312 | bytes 18883072 | tf_op jit(solution)/shard_map/oi,xiy->xoy/dot_general | solution.py:37
  169.9 7.5 %all_gather.7 = bf16[512,512]{0,1:T(8,128)(2,1)S(1)} all-gather(bf16[128,512]{0,1:T(8,128)(2,1)S(1)} %bitcast.285), channel_id=1, replica_groups=mesh['strip'=8,'col'=4] {'col'}, dimensions={0}, use_global_device_ids=true | all-gather | bytes 655360 | tf_op jit(solution)/shard_map/all_gather | solution.py:160
  177.4 1.5 fusion.60
  179.0 0.9 fusion.97
  (113 shorter events, 8.0 us)
Async XLA Ops:
  9.3 17.3 %copy-start.9 = (s32[1024,4]{0,1:T(4,128)S(1)}, s32[1024,4]{0,1:T(4,128)}, u32[]{:S(2)}) copy-start(s32[1024,4]{0,1:T(4,128)} %param.10) | copy-start | bytes 49156
  9.3 17.3 %copy-start.7 = (bf16[128,32,128]{2,1,0:T(8,128)(2,1)S(1)}, bf16[128,32,128]{2,1,0:T(8,128)(2,1)}, u32[]{:S(2)}) copy-start(bf16[128,32,128]{2,1,0:T(8,128)(2,1)} %param.17) | copy-start | bytes 3145732
  23.3 6.1 %collective-permute-start = (bf16[128,3,128]{0,2,1:T(8,128)(2,1)S(1)}, bf16[128,3,128]{0,2,1:T(8,128)(2,1)S(1)}, u32[]{:S(2)}, u32[]{:S(2)}) collective-permute-start(bf16[128,3,128]{0,2,1:T(8,128)(2,1)S(1)} %fusion.144), channel_id=1, source_target_pairs={{0,4},{4,8},{8,12},{12,16},{16,20},{20,24},{24,28},{1,5},{5,9},{9,... | collective-permute-start | bytes 294920 | tf_op jit(solution)/shard_map/ppermute | solution.py:11
  29.5 6.2 %collective-permute-start.2 = (bf16[128,35,2]{0,2,1:T(2,128)(2,1)S(1)}, bf16[128,35,2]{0,2,1:T(2,128)(2,1)S(1)}, u32[]{:S(2)}, u32[]{:S(2)}) collective-permute-start(bf16[128,35,2]{0,2,1:T(2,128)(2,1)S(1)} %get-tuple-element.87), channel_id=1, source_target_pairs={{4,0},{8,4},{12,8},{16,12},{20,16},{24,20},{28,24},{5,1},{9,5},{13... | collective-permute-start | bytes 53768 | tf_op jit(solution)/shard_map/ppermute | solution.py:22
  32.6 4.5 %collective-permute-start.1 = (bf16[128,35,2]{0,2,1:T(2,128)(2,1)S(1)}, bf16[128,35,2]{0,2,1:T(2,128)(2,1)S(1)}, u32[]{:S(2)}, u32[]{:S(2)}) collective-permute-start(bf16[128,35,2]{0,2,1:T(2,128)(2,1)S(1)} %get-tuple-element.86), channel_id=1, source_target_pairs={{0,4},{4,8},{8,12},{12,16},{16,20},{20,24},{24,28},{1,5},{5,9},{9,... | collective-permute-start | bytes 53768 | tf_op jit(solution)/shard_map/ppermute | solution.py:19
  35.7 14.2 %copy-start.10 = (bf16[3,3,32,3]{2,3,1,0:T(4,128)(2,1)S(1)}, bf16[3,3,32,3]{2,3,1,0:T(4,128)(2,1)}, u32[]{:S(2)}) copy-start(bf16[3,3,32,3]{2,3,1,0:T(4,128)(2,1)} %param.13) | copy-start | bytes 5188
  42.3 7.6 %collective-permute-start.3 = (bf16[2,35,132]{2,1,0:T(8,128)(2,1)S(1)}, bf16[2,35,132]{2,1,0:T(8,128)(2,1)S(1)}, u32[]{:S(2)}, u32[]{:S(2)}) collective-permute-start(bf16[2,35,132]{2,1,0:T(8,128)(2,1)S(1)} %get-tuple-element.84), channel_id=1, source_target_pairs={{0,1},{1,2},{2,3},{4,5},{5,6},{6,7},{8,9},{9,10},{10,11},{12,13},{... | collective-permute-start | bytes 55448 | tf_op jit(solution)/shard_map/ppermute | solution.py:19
  47.8 5.3 %collective-permute-start.4 = (bf16[2,35,132]{2,1,0:T(8,128)(2,1)S(1)}, bf16[2,35,132]{2,1,0:T(8,128)(2,1)S(1)}, u32[]{:S(2)}, u32[]{:S(2)}) collective-permute-start(bf16[2,35,132]{2,1,0:T(8,128)(2,1)S(1)} %get-tuple-element.85), channel_id=1, source_target_pairs={{1,0},{2,1},{3,2},{5,4},{6,5},{7,6},{9,8},{10,9},{11,10},{13,12},{... | collective-permute-start | bytes 55448 | tf_op jit(solution)/shard_map/ppermute | solution.py:22
  69.8 2.8 %copy-start.12 = (f32[32]{0:T(128)S(1)}, f32[32]{0:T(128)}, u32[]{:S(2)}) copy-start(f32[32]{0:T(128)} %param.14) | copy-start | bytes 388
  72.6 14.8 %copy-start.8 = (bf16[3,3,32,32]{3,2,1,0:T(8,128)(2,1)S(1)}, bf16[3,3,32,32]{3,2,1,0:T(8,128)(2,1)}, u32[]{:S(2)}) copy-start(bf16[3,3,32,32]{3,2,1,0:T(8,128)(2,1)} %param.15) | copy-start | bytes 55300
  129.4 36.0 %copy-start.5 = (f32[128,128,32]{1,2,0:T(8,128)S(1)}, f32[128,128,32]{1,2,0:T(8,128)}, u32[]{:S(2)}) copy-start(f32[128,128,32]{1,2,0:T(8,128)} %fusion.89) | copy-start | bytes 6291460
  129.4 36.0 %copy-start.6 = (f32[128,128,32]{1,2,0:T(8,128)S(1)}, f32[128,128,32]{1,2,0:T(8,128)}, u32[]{:S(2)}) copy-start(f32[128,128,32]{1,2,0:T(8,128)} %fusion.93) | copy-start | bytes 6291460
  146.8 18.6 %copy-start.4 = (f32[128,128,32]{1,2,0:T(8,128)S(1)}, f32[128,128,32]{1,2,0:T(8,128)}, u32[]{:S(2)}) copy-start(f32[128,128,32]{1,2,0:T(8,128)} %fusion.87) | copy-start | bytes 6291460
  149.0 16.3 %copy-start.3 = (f32[128,128,32]{1,2,0:T(8,128)S(1)}, f32[128,128,32]{1,2,0:T(8,128)}, u32[]{:S(2)}) copy-start(f32[128,128,32]{1,2,0:T(8,128)} %fusion.85) | copy-start | bytes 6291460
  153.4 12.0 %copy-start.2 = (f32[128,128,32]{1,2,0:T(8,128)S(1)}, f32[128,128,32]{1,2,0:T(8,128)}, u32[]{:S(2)}) copy-start(f32[128,128,32]{1,2,0:T(8,128)} %fusion.83) | copy-start | bytes 6291460
  155.6 9.8 %copy-start = (f32[128,128,32]{1,2,0:T(8,128)S(1)}, f32[128,128,32]{1,2,0:T(8,128)}, u32[]{:S(2)}) copy-start(f32[128,128,32]{1,2,0:T(8,128)} %fusion.79) | copy-start | bytes 6291460
  155.6 9.8 %copy-start.1 = (f32[128,128,32]{1,2,0:T(8,128)S(1)}, f32[128,128,32]{1,2,0:T(8,128)}, u32[]{:S(2)}) copy-start(f32[128,128,32]{1,2,0:T(8,128)} %fusion.81) | copy-start | bytes 6291460
  155.6 9.8 %copy-start.11 = (f32[32]{0:T(128)S(1)}, f32[32]{0:T(128)}, u32[]{:S(2)}) copy-start(f32[32]{0:T(128)} %param.16) | copy-start | bytes 388
  162.3 7.3 %collective-permute-start.5 = (bf16[128,2,128]{2,1,0:T(2,128)(2,1)S(1)}, bf16[128,2,128]{2,1,0:T(2,128)(2,1)S(1)}, u32[]{:S(2)}, u32[]{:S(2)}) collective-permute-start(bf16[128,2,128]{2,1,0:T(2,128)(2,1)S(1)} %bitcast.290), channel_id=1, source_target_pairs={{4,0},{8,4},{12,8},{16,12},{20,16},{24,20},{28,24},{5,1},{9,5},{13... | collective-permute-start | bytes 196616 | tf_op jit(solution)/shard_map/ppermute | solution.py:11
where the time goes:
time: 181 us; the launch traced here: 180 us
  matrix products  124 us (69%)
  starting transfers between devices  19.9 us (11%)
  blocking collectives  13.8 us (8%)
  local copies, waits for them, and re-layouts  9.63 us (5%)
  other arithmetic  7.78 us (4%)
  waiting for transfers between devices  3.59 us (2%)
    dot_general x18, matrix products, conv_back(): jnp.einsum('oi,xoy->xiy', weights[shift_row, shift_col], window, preferre...  59.7 us
    dot_general x18, matrix products, conv_valid(): jnp.einsum('oi,xiy->xoy', weights[shift_row, shift_col], window, preferre...  55.9 us
    ppermute x2, starting transfers between devices, with_halo(): lax.ppermute(lax.slice_in_dim(block, block.shape[dim] - width, None, axis...  8.54 us
    all_gather x1, blocking collectives, shards(): shard_piece = lax.all_gather(both_halves, 'col', axis=0, tiled=True)  7.48 us
    all_gather x1, blocking collectives, shards(): shard_piece = lax.all_gather(packed, 'col', axis=0, tiled=True)  6.3 us
    ppermute x2, starting transfers between devices, from_behind(): return lax.ppermute(x, axis, pairs)  6.19 us
    ppermute x2, starting transfers between devices, with_halo(): lax.ppermute(lax.slice_in_dim(block, 0, width, axis=dim), axis, backward)  5.17 us
    dot_general x4, matrix products, column_block(): jnp.einsum('pk,phr->khr', pin_cols, pin_factor, preferred_element_type=jn...  4.31 us
  transfers between devices with their start and end apart: 6, of which 3 were waited for; matrix products, arithmetic and copies ran while one was open for 4% of the time, Pallas kernels for 0%

commit v1 on v0

--- a/solution.py
+++ b/solution.py
@@ -157,7 +157,14 @@
     both_halves = jnp.stack([back_maps, from_below], axis=1).reshape(tile_cols, 4 * span)
     left_col = net_box[:, 0]
     right_col = net_box[:, 1]
-    shard_piece = lax.all_gather(both_halves, "col", axis=0, tiled=True)
+    ways, here = (lax.axis_size("col"), lax.axis_index("col"))
+    shard_piece, reach = (both_halves, 1)
+    while reach < ways:
+        theirs = lax.ppermute(shard_piece, "col", [(d, d ^ reach) for d in range(ways)])
+        mine_first = jnp.concatenate([shard_piece, theirs], axis=0)
+        theirs_first = jnp.concatenate([theirs, shard_piece], axis=0)
+        shard_piece = jnp.where(here & reach == 0, mine_first, theirs_first)
+        reach = 2 * reach
     piece_cols = jnp.arange(shard_piece.shape[0], dtype=jnp.int32)
     net_cols = (
         (left_col[:, None] <= piece_cols[None, :]) & (piece_cols[None, :] <= right_col[:, None])

time: 181 us -> 164 us (0.906)
  matrix products: 124 us -> 111 us
  blocking collectives: 13.8 us -> 6.3 us
  starting transfers between devices: 19.9 us -> 22.4 us
    dot_general x18, matrix products: 59.7 us -> 44.4 us  [conv_back(): jnp.einsum('oi,xoy->xiy', weights[shift_row, shift_col], window, preferre...]
    all_gather x1 -> x0, blocking collectives: 7.48 us -> none  [shards(): shard_piece = lax.all_gather(both_halves, 'col', axis=0, tiled=True)]
    dot_general x18, matrix products: 55.9 us -> 59 us  [conv_valid(): jnp.einsum('oi,xiy->xoy', weights[shift_row, shift_col], window, preferre...]
    ppermute x0 -> x2, starting transfers between devices: none -> 2.54 us  [shards(): lax.ppermute(shard_piece, 'col', [(d, d ^ reach) for d in range(ways)])]
  transfers between devices with their start and end apart: 6 -> 8, of which waited for: 3 -> 4; matrix products, arithmetic and copies ran while one was open for 4% -> 9% of each run, Pallas kernels for 0% -> 0%
where the time goes in v1:
time: 164 us
  matrix products  111 us (68%)
  starting transfers between devices  22.4 us (14%)
  local copies, waits for them, and re-layouts  9.61 us (6%)
  other arithmetic  7.9 us (5%)
  blocking collectives  6.3 us (4%)
  waiting for transfers between devices  4.73 us (3%)
    dot_general x18, matrix products, conv_valid(): jnp.einsum('oi,xiy->xoy', weights[shift_row, shift_col], window, preferre...  59 us
    dot_general x18, matrix products, conv_back(): jnp.einsum('oi,xoy->xiy', weights[shift_row, shift_col], window, preferre...  44.4 us
    ppermute x2, starting transfers between devices, with_halo(): lax.ppermute(lax.slice_in_dim(block, block.shape[dim] - width, None, axis...  8.55 us
    all_gather x1, blocking collectives, shards(): shard_piece = lax.all_gather(packed, 'col', axis=0, tiled=True)  6.3 us
    ppermute x2, starting transfers between devices, from_behind(): return lax.ppermute(x, axis, pairs)  6.18 us
    ppermute x2, starting transfers between devices, with_halo(): lax.ppermute(lax.slice_in_dim(block, 0, width, axis=dim), axis, backward)  5.17 us
    dot_general x4, matrix products, column_block(): jnp.einsum('pk,phr->khr', pin_cols, pin_factor, preferred_element_type=jn...  4.31 us
    concatenate x1, local copies, waits for them, and re-layouts, with_halo(): block = jnp.concatenate([low, block, high], axis=dim)  3.6 us
  transfers between devices with their start and end apart: 8, of which 4 were waited for; matrix products, arithmetic and copies ran while one was open for 9% of the time, Pallas kernels for 0%

profile of v1, /device:TPU:19, one launch (start us, length us, event | category | flops | bytes accessed | tf_op | source)
XLA Modules:
  0.0 163.7 jit_solution(18188064012344319711)
XLA Ops:
  0.6 0.8 convert_element_type.81
  1.5 0.7 convert_element_type.80
  2.2 0.7 pad_maximum_fusion.10
  2.9 6.3 %all_gather.3 = f32[4096,13]{0,1:T(8,128)S(1)} all-gather(f32[1024,13]{0,1:T(8,128)S(1)} %pad_maximum_fusion.10), channel_id=1, replica_groups=mesh['strip'=8,'col'=4] {'col'}, dimensions={0}, use_global_device_ids=true | all-gather | bytes 266240 | tf_op jit(solution)/shard_map/all_gather | solution.py:112
  9.4 13.7 %while.11 = (s32[]{:T(128)}, f32[128,2,3,128]{3,0,2,1:T(8,128)S(1)}, f32[4,1024,13]{1,0,2:T(4,128)S(1)}, s32[]{:T(128)}, s32[]{:T(128)}, /*index=5*/s32[]{:T(128)}, s32[]{:T(128)}) while((s32[]{:T(128)}, f32[128,2,3,128]{3,0,2,1:T(8,128)S(1)}, f32[4,1024,13]{1,0,2:T(4,128)S(1)}, s32[]{:T(128)}, s32[]{:T(128)}, ...), condition=%wide.region_1.2_spmd.clone, body=%wide.region_0.1_spmd.clone.sunk | while | flops 408091520 | bytes 3318379 | solution.py:134
  10.6 1.1 fusion.257
  11.8 0.3 and_convert_fusion.2
  12.1 0.5 fusion.260
  14.0 1.1 fusion.257
  15.5 0.5 fusion.260
  17.4 1.1 fusion.257
  19.0 0.5 fusion.260
  20.9 1.1 fusion.257
  22.4 0.5 fusion.260
  23.3 3.2 %collective-permute-start = (bf16[128,3,128]{0,2,1:T(8,128)(2,1)S(1)}, bf16[128,3,128]{0,2,1:T(8,128)(2,1)S(1)}, u32[]{:S(2)}, u32[]{:S(2)}) collective-permute-start(bf16[128,3,128]{0,2,1:T(8,128)(2,1)S(1)} %fusion.150), channel_id=1, source_target_pairs={{0,4},{4,8},{8,12},{12,16},{16,20},{20,24},{24,28},{1,5},{5,9},{9,... | collective-permute-start | bytes 294920 | tf_op jit(solution)/shard_map/ppermute | solution.py:11
  26.6 1.0 copy.57
  27.6 1.8 %collective-permute-done = bf16[128,3,128]{0,2,1:T(8,128)(2,1)S(1)} collective-permute-done((bf16[128,3,128]{0,2,1:T(8,128)(2,1)S(1)}, bf16[128,3,128]{0,2,1:T(8,128)(2,1)S(1)}, u32[]{:S(2)}, u32[]{:S(2)}) %collective-permute-start) | collective-permute-done | bytes 98336 | tf_op jit(solution)/shard_map/ppermute | solution.py:11
  29.5 3.1 %collective-permute-start.2 = (bf16[128,35,2]{0,2,1:T(2,128)(2,1)S(1)}, bf16[128,35,2]{0,2,1:T(2,128)(2,1)S(1)}, u32[]{:S(2)}, u32[]{:S(2)}) collective-permute-start(bf16[128,35,2]{0,2,1:T(2,128)(2,1)S(1)} %get-tuple-element.87), channel_id=1, source_target_pairs={{4,0},{8,4},{12,8},{16,12},{20,16},{24,20},{28,24},{5,1},{9,5},{13... | collective-permute-start | bytes 53768 | tf_op jit(solution)/shard_map/ppermute | solution.py:22
  32.6 3.1 %collective-permute-start.1 = (bf16[128,35,2]{0,2,1:T(2,128)(2,1)S(1)}, bf16[128,35,2]{0,2,1:T(2,128)(2,1)S(1)}, u32[]{:S(2)}, u32[]{:S(2)}) collective-permute-start(bf16[128,35,2]{0,2,1:T(2,128)(2,1)S(1)} %get-tuple-element.86), channel_id=1, source_target_pairs={{0,4},{4,8},{8,12},{12,16},{16,20},{20,24},{24,28},{1,5},{5,9},{9,... | collective-permute-start | bytes 53768 | tf_op jit(solution)/shard_map/ppermute | solution.py:19
  35.7 1.3 collective-permute-done.1
  37.1 1.6 pad_maximum_fusion.8
  38.7 3.6 %copy.58 = bf16[128,35,132]{2,1,0:T(8,128)(2,1)S(1)} copy(bf16[128,35,132]{0,2,1:T(8,128)(2,1)} %pad_maximum_fusion.8) | data formatting | bytes 2365440 | tf_op jit(solution)/shard_map/concatenate | solution.py:23
  42.3 5.4 %collective-permute-start.3 = (bf16[2,35,132]{2,1,0:T(8,128)(2,1)S(1)}, bf16[2,35,132]{2,1,0:T(8,128)(2,1)S(1)}, u32[]{:S(2)}, u32[]{:S(2)}) collective-permute-start(bf16[2,35,132]{2,1,0:T(8,128)(2,1)S(1)} %get-tuple-element.84), channel_id=1, source_target_pairs={{0,1},{1,2},{2,3},{4,5},{5,6},{6,7},{8,9},{9,10},{10,11},{12,13},{... | collective-permute-start | bytes 55448 | tf_op jit(solution)/shard_map/ppermute | solution.py:19
  47.8 2.1 %collective-permute-start.4 = (bf16[2,35,132]{2,1,0:T(8,128)(2,1)S(1)}, bf16[2,35,132]{2,1,0:T(8,128)(2,1)S(1)}, u32[]{:S(2)}, u32[]{:S(2)}) collective-permute-start(bf16[2,35,132]{2,1,0:T(8,128)(2,1)S(1)} %get-tuple-element.85), channel_id=1, source_target_pairs={{1,0},{2,1},{3,2},{5,4},{6,5},{7,6},{9,8},{10,9},{11,10},{13,12},{... | collective-permute-start | bytes 55448 | tf_op jit(solution)/shard_map/ppermute | solution.py:22
  49.9 2.7 %fusion.116 = f32[130,130,32]{1,2,0:T(8,128)} fusion(bf16[128,35,132]{2,1,0:T(8,128)(2,1)S(1)} %copy.58, bf16[2,35,132]{2,1,0:T(8,128)(2,1)S(1)} %collective-permute-done.3, bf16[3,3,32,3]{2,3,1,0:T(4,128)(2,1)S(1)} %copy-done.6), kind=kOutput, calls=%fused_computation.146 | convolution fusion | flops 3447600 | bytes 4826624 | tf_op jit(solution)/shard_map/oi,xiy->xoy/dot_general | solution.py:37
  52.7 0.5 collective-permute-done.4
  53.1 2.9 %fusion.110 = f32[130,130,32]{1,2,0:T(8,128)} fusion(bf16[2,35,132]{2,1,0:T(8,128)(2,1)S(1)} %collective-permute-done.4, bf16[128,35,132]{2,1,0:T(8,128)(2,1)S(1)} %copy.58, bf16[2,35,132]{2,1,0:T(8,128)(2,1)S(1)} %collective-permute-done.3, bf16[3,3,32,3]{2,3,1,0:T(4,128)(2,1)S(1)} %copy-done.6), kind=kOutput, calls=%fused_computation.140 | convolution fusion | flops 3549000 | bytes 4867584 | tf_op jit(solution)/shard_map/oi,xiy->xoy/dot_general | solution.py:37
  56.0 2.8 %fusion.120 = f32[130,130,32]{1,2,0:T(8,128)} fusion(bf16[2,35,132]{2,1,0:T(8,128)(2,1)S(1)} %collective-permute-done.4, bf16[128,35,132]{2,1,0:T(8,128)(2,1)S(1)} %copy.58, bf16[3,3,32,3]{2,3,1,0:T(4,128)(2,1)S(1)} %copy-done.6), kind=kOutput, calls=%fused_computation.150 | convolution fusion | flops 3447600 | bytes 4826624 | tf_op jit(solution)/shard_map/oi,xiy->xoy/dot_general | solution.py:37
  58.8 2.8 %fusion.124 = f32[130,130,32]{1,2,0:T(8,128)} fusion(bf16[2,35,132]{2,1,0:T(8,128)(2,1)S(1)} %collective-permute-done.4, bf16[128,35,132]{2,1,0:T(8,128)(2,1)S(1)} %copy.58, bf16[2,35,132]{2,1,0:T(8,128)(2,1)S(1)} %collective-permute-done.3, bf16[3,3,32,3]{2,3,1,0:T(4,128)(2,1)S(1)} %copy-done.6), kind=kOutput, calls=%fused_computation.154 | convolution fusion | flops 3549000 | bytes 4867584 | tf_op jit(solution)/shard_map/oi,xiy->xoy/dot_general | solution.py:37
  61.6 2.7 %fusion.130 = f32[130,130,32]{1,2,0:T(8,128)} fusion(bf16[128,35,132]{2,1,0:T(8,128)(2,1)S(1)} %copy.58, bf16[2,35,132]{2,1,0:T(8,128)(2,1)S(1)} %collective-permute-done.3, bf16[3,3,32,3]{2,3,1,0:T(4,128)(2,1)S(1)} %copy-done.6), kind=kOutput, calls=%fused_computation.160 | convolution fusion | flops 3447600 | bytes 4826624 | tf_op jit(solution)/shard_map/oi,xiy->xoy/dot_general | solution.py:37
  64.3 2.7 %fusion.134 = f32[130,130,32]{1,2,0:T(8,128)} fusion(bf16[2,35,132]{2,1,0:T(8,128)(2,1)S(1)} %collective-permute-done.4, bf16[128,35,132]{2,1,0:T(8,128)(2,1)S(1)} %copy.58, bf16[3,3,32,3]{2,3,1,0:T(4,128)(2,1)S(1)} %copy-done.6), kind=kOutput, calls=%fused_computation.164 | convolution fusion | flops 3447600 | bytes 4826624 | tf_op jit(solution)/shard_map/oi,xiy->xoy/dot_general | solution.py:37
  67.1 2.8 %fusion.144 = f32[130,130,32]{1,2,0:T(8,128)} fusion(bf16[128,35,132]{2,1,0:T(8,128)(2,1)S(1)} %copy.58, bf16[2,35,132]{2,1,0:T(8,128)(2,1)S(1)} %collective-permute-done.3, bf16[3,3,32,3]{2,3,1,0:T(4,128)(2,1)S(1)} %copy-done.6), kind=kOutput, calls=%fused_computation.174 | convolution fusion | flops 3447600 | bytes 4826624 | tf_op jit(solution)/shard_map/oi,xiy->xoy/dot_general | solution.py:37
  69.9 2.8 %fusion.138 = f32[130,130,32]{1,2,0:T(8,128)} fusion(bf16[2,35,132]{2,1,0:T(8,128)(2,1)S(1)} %collective-permute-done.4, bf16[128,35,132]{2,1,0:T(8,128)(2,1)S(1)} %copy.58, bf16[2,35,132]{2,1,0:T(8,128)(2,1)S(1)} %collective-permute-done.3, bf16[3,3,32,3]{2,3,1,0:T(4,128)(2,1)S(1)} %copy-done.6), kind=kOutput, calls=%fused_computation.168 | convolution fusion | flops 3549000 | bytes 4867584 | tf_op jit(solution)/shard_map/oi,xiy->xoy/dot_general | solution.py:37
  72.7 14.8 %fusion.34 = (bf16[130,32,130]{2,1,0:T(8,128)(2,1)S(1)}, f32[130,130,32]{1,2,0:T(8,128)}) fusion(pred[130,130]{1,0:T(8,128)(4,1)S(1)} %broadcast_and_fusion, f32[32]{0:T(128)S(1)} %copy-done.8, bf16[3,3,32,3]{2,3,1,0:T(4,128)(2,1)S(1)} %copy-done.6, bf16[2,35,132]{2,1,0:T(8,128)(2,1)S(1)} %collective-permute-done.4, bf16[128,35,132]{2,1,0:T(8,128)(2,1)S(1)} %copy.58, ...), kind=kOutput, calls=%fused_computation.44 | convolution fusion | flops 11559600 | bytes 23249152 | tf_op jit(solution)/shard_map/oi,xiy->xoy/dot_general | solution.py:37
  87.5 2.0 %fusion.79 = f32[128,128,32]{1,2,0:T(8,128)} fusion(bf16[130,32,130]{2,1,0:T(8,128)(2,1)S(1)} %get-tuple-element.92, bf16[3,3,32,32]{3,2,1,0:T(8,128)(2,1)S(1)} %copy-done.4), kind=kOutput, calls=%fused_computation.110 | convolution fusion | flops 33554432 | bytes 3153920 | tf_op jit(solution)/shard_map/oi,xiy->xoy/dot_general | solution.py:37
  89.5 1.8 %fusion.81 = f32[128,128,32]{1,2,0:T(8,128)} fusion(bf16[130,32,130]{2,1,0:T(8,128)(2,1)S(1)} %get-tuple-element.92, bf16[3,3,32,32]{3,2,1,0:T(8,128)(2,1)S(1)} %copy-done.4), kind=kOutput, calls=%fused_computation.112 | convolution fusion | flops 33554432 | bytes 3153920 | tf_op jit(solution)/shard_map/oi,xiy->xoy/dot_general | solution.py:37
  91.3 1.9 %fusion.83 = f32[128,128,32]{1,2,0:T(8,128)} fusion(bf16[130,32,130]{2,1,0:T(8,128)(2,1)S(1)} %get-tuple-element.92, bf16[3,3,32,32]{3,2,1,0:T(8,128)(2,1)S(1)} %copy-done.4), kind=kOutput, calls=%fused_computation.114 | convolution fusion | flops 33554432 | bytes 3153920 | tf_op jit(solution)/shard_map/oi,xiy->xoy/dot_general | solution.py:37
  93.2 1.9 %fusion.85 = f32[128,128,32]{1,2,0:T(8,128)} fusion(bf16[130,32,130]{2,1,0:T(8,128)(2,1)S(1)} %get-tuple-element.92, bf16[3,3,32,32]{3,2,1,0:T(8,128)(2,1)S(1)} %copy-done.4), kind=kOutput, calls=%fused_computation.116 | convolution fusion | flops 33554432 | bytes 3153920 | tf_op jit(solution)/shard_map/oi,xiy->xoy/dot_general | solution.py:37
  95.1 1.9 %fusion.87 = f32[128,128,32]{1,2,0:T(8,128)} fusion(bf16[130,32,130]{2,1,0:T(8,128)(2,1)S(1)} %get-tuple-element.92, bf16[3,3,32,32]{3,2,1,0:T(8,128)(2,1)S(1)} %copy-done.4), kind=kOutput, calls=%fused_computation.118 | convolution fusion | flops 33554432 | bytes 3153920 | tf_op jit(solution)/shard_map/oi,xiy->xoy/dot_general | solution.py:37
  97.0 1.7 %fusion.89 = f32[128,128,32]{1,2,0:T(8,128)} fusion(bf16[130,32,130]{2,1,0:T(8,128)(2,1)S(1)} %get-tuple-element.92, bf16[3,3,32,32]{3,2,1,0:T(8,128)(2,1)S(1)} %copy-done.4), kind=kOutput, calls=%fused_computation.120 | convolution fusion | flops 33554432 | bytes 3153920 | tf_op jit(solution)/shard_map/oi,xiy->xoy/dot_general | solution.py:37
  98.7 0.6 pad_maximum_fusion.1
  99.3 2.7 %fusion.51 = f32[130,130,32]{1,2,0:T(8,128)} fusion(bf16[132,35,132]{2,1,0:T(8,128)(2,1)S(1)} %pad_maximum_fusion.1, bf16[3,3,32,32]{3,2,1,0:T(8,128)(2,1)S(1)} %copy-done.4), kind=kOutput, calls=%fused_computation.68 | convolution fusion | flops 34611200 | bytes 4301312 | tf_op jit(solution)/shard_map/oi,xoy->xiy/dot_general | solution.py:56
  102.0 3.2 %fusion.55 = f32[130,130,32]{1,2,0:T(8,128)} fusion(bf16[132,35,132]{2,1,0:T(8,128)(2,1)S(1)} %pad_maximum_fusion.1, bf16[3,3,32,32]{3,2,1,0:T(8,128)(2,1)S(1)} %copy-done.4), kind=kOutput, calls=%fused_computation.73 | convolution fusion | flops 34611200 | bytes 4301312 | tf_op jit(solution)/shard_map/oi,xoy->xiy/dot_general | solution.py:56
  105.2 3.2 %fusion.57 = f32[130,130,32]{1,2,0:T(8,128)} fusion(bf16[132,35,132]{2,1,0:T(8,128)(2,1)S(1)} %pad_maximum_fusion.1, bf16[3,3,32,32]{3,2,1,0:T(8,128)(2,1)S(1)} %copy-done.4), kind=kOutput, calls=%fused_computation.75 | convolution fusion | flops 34611200 | bytes 4301312 | tf_op jit(solution)/shard_map/oi,xoy->xiy/dot_general | solution.py:56
  108.3 2.8 %fusion.53 = f32[130,130,32]{1,2,0:T(8,128)} fusion(bf16[2,35,132]{2,1,0:T(8,128)(2,1)S(1)} %collective-permute-done.4, bf16[128,35,132]{2,1,0:T(8,128)(2,1)S(1)} %copy.58, bf16[3,3,32,32]{3,2,1,0:T(8,128)(2,1)S(1)} %copy-done.4), kind=kOutput, calls=%fused_computation.71 | convolution fusion | flops 36774400 | bytes 4833792 | tf_op jit(solution)/shard_map/oi,xoy->xiy/dot_general | solution.py:56
  111.2 3.7 %fusion.44 = f32[130,130,32]{1,2,0:T(8,128)} fusion(bf16[128,35,132]{2,1,0:T(8,128)(2,1)S(1)} %copy.58, bf16[2,35,132]{2,1,0:T(8,128)(2,1)S(1)} %collective-permute-done.3, bf16[3,3,32,32]{3,2,1,0:T(8,128)(2,1)S(1)} %copy-done.4), kind=kOutput, calls=%fused_computation.62 | convolution fusion | flops 35152000 | bytes 4833792 | tf_op jit(solution)/shard_map/oi,xoy->xiy/dot_general | solution.py:56
  114.8 3.6 %fusion.38 = f32[130,130,32]{1,2,0:T(8,128)} fusion(bf16[128,35,132]{2,1,0:T(8,128)(2,1)S(1)} %copy.58, bf16[2,35,132]{2,1,0:T(8,128)(2,1)S(1)} %collective-permute-done.4, bf16[3,3,32,32]{3,2,1,0:T(8,128)(2,1)S(1)} %copy-done.4), kind=kOutput, calls=%fused_computation.58 | convolution fusion | flops 35152000 | bytes 4833792 | tf_op jit(solution)/shard_map/oi,xoy->xiy/dot_general | solution.py:56
  118.4 4.0 %fusion.47 = f32[130,130,32]{1,2,0:T(8,128)} fusion(bf16[128,35,132]{2,1,0:T(8,128)(2,1)S(1)} %copy.58, bf16[2,35,132]{2,1,0:T(8,128)(2,1)S(1)} %collective-permute-done.3, bf16[3,3,32,32]{3,2,1,0:T(8,128)(2,1)S(1)} %copy-done.4), kind=kOutput, calls=%fused_computation.64 | convolution fusion | flops 35152000 | bytes 4833792 | tf_op jit(solution)/shard_map/oi,xoy->xiy/dot_general | solution.py:56
  122.4 3.7 %fusion.41 = f32[130,130,32]{1,2,0:T(8,128)} fusion(bf16[128,35,132]{2,1,0:T(8,128)(2,1)S(1)} %copy.58, bf16[2,35,132]{2,1,0:T(8,128)(2,1)S(1)} %collective-permute-done.4, bf16[3,3,32,32]{3,2,1,0:T(8,128)(2,1)S(1)} %copy-done.4), kind=kOutput, calls=%fused_computation.60 | convolution fusion | flops 35152000 | bytes 4833792 | tf_op jit(solution)/shard_map/oi,xoy->xiy/dot_general | solution.py:56
  126.1 13.8 %fusion.29 = bf16[130,32,130]{2,1,0:T(8,128)(2,1)S(1)} fusion(f32[130,130,32]{1,2,0:T(8,128)} %get-tuple-element.93, f32[130,130,32]{1,2,0:T(8,128)} %fusion.51, f32[130,130,32]{1,2,0:T(8,128)} %fusion.53, f32[130,130,32]{1,2,0:T(8,128)} %fusion.44, f32[130,130,32]{1,2,0:T(8,128)} %fusion.55, f32[130,130,32]{1,2,0:T(8,128)} %fusion.38, ...), kind=kOutput, calls=%fused_computation.36 | convolution fusion | flops 46508800 | bytes 23255808 | tf_op jit(solution)/shard_map/oi,xoy->xiy/dot_general | solution.py:56
  140.0 0.5 fusion.76
  140.5 0.5 convolution_add_fusion.7
  141.0 0.5 convolution_add_fusion.6
  141.5 0.5 convolution_add_fusion.5
  142.0 0.5 convolution_add_fusion.4
  142.5 0.5 convolution_add_fusion.3
  143.7 3.0 %collective-permute-start.5 = (bf16[128,2,128]{2,1,0:T(2,128)(2,1)S(1)}, bf16[128,2,128]{2,1,0:T(2,128)(2,1)S(1)}, u32[]{:S(2)}, u32[]{:S(2)}) collective-permute-start(bf16[128,2,128]{2,1,0:T(2,128)(2,1)S(1)} %bitcast.290), channel_id=1, source_target_pairs={{4,0},{8,4},{12,8},{16,12},{20,16},{24,20},{28,24},{5,1},{9,5},{13... | collective-permute-start | bytes 196616 | tf_op jit(solution)/shard_map/ppermute | solution.py:11
  146.8 1.8 %fusion.93 = f32[128,128,32]{1,2,0:T(8,128)} fusion(bf16[130,32,130]{2,1,0:T(8,128)(2,1)S(1)} %get-tuple-element.92, bf16[3,3,32,32]{3,2,1,0:T(8,128)(2,1)S(1)} %copy-done.4), kind=kOutput, calls=%fused_computation.124 | convolution fusion | flops 33554432 | bytes 3153920 | tf_op jit(solution)/shard_map/oi,xiy->xoy/dot_general | solution.py:37
  148.5 1.1 collective-permute-done.5
  150.1 1.8 %fusion.91 = f32[128,128,32]{1,2,0:T(8,128)S(1)} fusion(bf16[130,32,130]{2,1,0:T(8,128)(2,1)} %copy-done, bf16[3,3,32,32]{3,2,1,0:T(8,128)(2,1)S(1)} %copy-done.4), kind=kOutput, calls=%fused_computation.122 | convolution fusion | flops 33554432 | bytes 3153920 | tf_op jit(solution)/shard_map/oi,xiy->xoy/dot_general | solution.py:37
  151.9 2.5 %collective-permute-start.7 = (bf16[256,512]{0,1:T(8,128)(2,1)S(1)}, bf16[256,512]{0,1:T(8,128)(2,1)S(1)}, u32[]{:S(2)}, u32[]{:S(2)}) collective-permute-start(bf16[256,512]{0,1:T(8,128)(2,1)S(1)} %maximum_select_fusion.2), channel_id=1, source_target_pairs={{0,2},{1,3},{2,0},{3,1},{4,6},{5,7},{6,4},{7,5},{8,10},{9,11},{10,... | collective-permute-start | bytes 786440 | tf_op jit(solution)/shard_map/ppermute | solution.py:163
  154.4 7.2 %fusion.62 = bf16[128,32,128]{2,1,0:T(8,128)(2,1)} fusion(f32[128,128,32]{1,2,0:T(8,128)S(1)} %copy-done.1, f32[128,128,32]{1,2,0:T(8,128)S(1)} %copy-done.2, f32[128,128,32]{1,2,0:T(8,128)} %fusion.83, f32[128,128,32]{1,2,0:T(8,128)} %fusion.85, f32[128,128,32]{1,2,0:T(8,128)} %fusion.87, f32[128,128,32]{1,2,0:T(8,128)} %fusion.89, ...), kind=kOutput, calls=%fused_computation.82 | convolution fusion | flops 38797312 | bytes 18883072 | tf_op jit(solution)/shard_map/oi,xiy->xoy/dot_general | solution.py:37
  161.6 1.1 fusion.60
  162.8 0.9 fusion.97
  (109 shorter events, 8.1 us)
Async XLA Ops:
  9.3 17.3 %copy-start.5 = (s32[1024,4]{0,1:T(4,128)S(1)}, s32[1024,4]{0,1:T(4,128)}, u32[]{:S(2)}) copy-start(s32[1024,4]{0,1:T(4,128)} %param.10) | copy-start | bytes 49156
  9.3 17.3 %copy-start.3 = (bf16[128,32,128]{2,1,0:T(8,128)(2,1)S(1)}, bf16[128,32,128]{2,1,0:T(8,128)(2,1)}, u32[]{:S(2)}) copy-start(bf16[128,32,128]{2,1,0:T(8,128)(2,1)} %param.17) | copy-start | bytes 3145732
  23.3 6.1 %collective-permute-start = (bf16[128,3,128]{0,2,1:T(8,128)(2,1)S(1)}, bf16[128,3,128]{0,2,1:T(8,128)(2,1)S(1)}, u32[]{:S(2)}, u32[]{:S(2)}) collective-permute-start(bf16[128,3,128]{0,2,1:T(8,128)(2,1)S(1)} %fusion.150), channel_id=1, source_target_pairs={{0,4},{4,8},{8,12},{12,16},{16,20},{20,24},{24,28},{1,5},{5,9},{9,... | collective-permute-start | bytes 294920 | tf_op jit(solution)/shard_map/ppermute | solution.py:11
  29.5 6.2 %collective-permute-start.2 = (bf16[128,35,2]{0,2,1:T(2,128)(2,1)S(1)}, bf16[128,35,2]{0,2,1:T(2,128)(2,1)S(1)}, u32[]{:S(2)}, u32[]{:S(2)}) collective-permute-start(bf16[128,35,2]{0,2,1:T(2,128)(2,1)S(1)} %get-tuple-element.87), channel_id=1, source_target_pairs={{4,0},{8,4},{12,8},{16,12},{20,16},{24,20},{28,24},{5,1},{9,5},{13... | collective-permute-start | bytes 53768 | tf_op jit(solution)/shard_map/ppermute | solution.py:22
  32.6 4.5 %collective-permute-start.1 = (bf16[128,35,2]{0,2,1:T(2,128)(2,1)S(1)}, bf16[128,35,2]{0,2,1:T(2,128)(2,1)S(1)}, u32[]{:S(2)}, u32[]{:S(2)}) collective-permute-start(bf16[128,35,2]{0,2,1:T(2,128)(2,1)S(1)} %get-tuple-element.86), channel_id=1, source_target_pairs={{0,4},{4,8},{8,12},{12,16},{16,20},{20,24},{24,28},{1,5},{5,9},{9,... | collective-permute-start | bytes 53768 | tf_op jit(solution)/shard_map/ppermute | solution.py:19
  35.7 14.2 %copy-start.6 = (bf16[3,3,32,3]{2,3,1,0:T(4,128)(2,1)S(1)}, bf16[3,3,32,3]{2,3,1,0:T(4,128)(2,1)}, u32[]{:S(2)}) copy-start(bf16[3,3,32,3]{2,3,1,0:T(4,128)(2,1)} %param.13) | copy-start | bytes 5188
  42.3 7.6 %collective-permute-start.3 = (bf16[2,35,132]{2,1,0:T(8,128)(2,1)S(1)}, bf16[2,35,132]{2,1,0:T(8,128)(2,1)S(1)}, u32[]{:S(2)}, u32[]{:S(2)}) collective-permute-start(bf16[2,35,132]{2,1,0:T(8,128)(2,1)S(1)} %get-tuple-element.84), channel_id=1, source_target_pairs={{0,1},{1,2},{2,3},{4,5},{5,6},{6,7},{8,9},{9,10},{10,11},{12,13},{... | collective-permute-start | bytes 55448 | tf_op jit(solution)/shard_map/ppermute | solution.py:19
  47.8 5.3 %collective-permute-start.4 = (bf16[2,35,132]{2,1,0:T(8,128)(2,1)S(1)}, bf16[2,35,132]{2,1,0:T(8,128)(2,1)S(1)}, u32[]{:S(2)}, u32[]{:S(2)}) collective-permute-start(bf16[2,35,132]{2,1,0:T(8,128)(2,1)S(1)} %get-tuple-element.85), channel_id=1, source_target_pairs={{1,0},{2,1},{3,2},{5,4},{6,5},{7,6},{9,8},{10,9},{11,10},{13,12},{... | collective-permute-start | bytes 55448 | tf_op jit(solution)/shard_map/ppermute | solution.py:22
  69.8 2.8 %copy-start.8 = (f32[32]{0:T(128)S(1)}, f32[32]{0:T(128)}, u32[]{:S(2)}) copy-start(f32[32]{0:T(128)} %param.14) | copy-start | bytes 388
  72.7 14.8 %copy-start.4 = (bf16[3,3,32,32]{3,2,1,0:T(8,128)(2,1)S(1)}, bf16[3,3,32,32]{3,2,1,0:T(8,128)(2,1)}, u32[]{:S(2)}) copy-start(bf16[3,3,32,32]{3,2,1,0:T(8,128)(2,1)} %param.15) | copy-start | bytes 55300
  87.5 59.3 %copy-start = (bf16[130,32,130]{2,1,0:T(8,128)(2,1)}, bf16[130,32,130]{2,1,0:T(8,128)(2,1)S(1)}, u32[]{:S(2)}) copy-start(bf16[130,32,130]{2,1,0:T(8,128)(2,1)S(1)} %get-tuple-element.92) | copy-start | bytes 3244804
  143.7 5.9 %collective-permute-start.5 = (bf16[128,2,128]{2,1,0:T(2,128)(2,1)S(1)}, bf16[128,2,128]{2,1,0:T(2,128)(2,1)S(1)}, u32[]{:S(2)}, u32[]{:S(2)}) collective-permute-start(bf16[128,2,128]{2,1,0:T(2,128)(2,1)S(1)} %bitcast.290), channel_id=1, source_target_pairs={{4,0},{8,4},{12,8},{16,12},{20,16},{24,20},{28,24},{5,1},{9,5},{13... | collective-permute-start | bytes 196616 | tf_op jit(solution)/shard_map/ppermute | solution.py:11
  148.5 5.9 %copy-start.1 = (f32[128,128,32]{1,2,0:T(8,128)S(1)}, f32[128,128,32]{1,2,0:T(8,128)}, u32[]{:S(2)}) copy-start(f32[128,128,32]{1,2,0:T(8,128)} %fusion.79) | copy-start | bytes 6291460
  148.5 5.9 %copy-start.7 = (f32[32]{0:T(128)S(1)}, f32[32]{0:T(128)}, u32[]{:S(2)}) copy-start(f32[32]{0:T(128)} %param.16) | copy-start | bytes 388
  150.0 4.4 %copy-start.2 = (f32[128,128,32]{1,2,0:T(8,128)S(1)}, f32[128,128,32]{1,2,0:T(8,128)}, u32[]{:S(2)}) copy-start(f32[128,128,32]{1,2,0:T(8,128)} %fusion.81) | copy-start | bytes 6291460
  150.0 1.9 %collective-permute-start.6 = (bf16[128,512]{0,1:T(8,128)(2,1)S(1)}, bf16[128,512]{0,1:T(8,128)(2,1)S(1)}, u32[]{:S(2)}, u32[]{:S(2)}) collective-permute-start(bf16[128,512]{0,1:T(8,128)(2,1)S(1)} %bitcast.284), channel_id=1, source_target_pairs={{0,1},{1,0},{2,3},{3,2},{4,5},{5,4},{6,7},{7,6},{8,9},{9,8},{10,11... | collective-permute-start | bytes 393224 | tf_op jit(solution)/shard_map/ppermute | solution.py:163
  151.9 9.7 %collective-permute-start.7 = (bf16[256,512]{0,1:T(8,128)(2,1)S(1)}, bf16[256,512]{0,1:T(8,128)(2,1)S(1)}, u32[]{:S(2)}, u32[]{:S(2)}) collective-permute-start(bf16[256,512]{0,1:T(8,128)(2,1)S(1)} %maximum_select_fusion.2), channel_id=1, source_target_pairs={{0,2},{1,3},{2,0},{3,1},{4,6},{5,7},{6,4},{7,5},{8,10},{9,11},{10,... | collective-permute-start | bytes 786440 | tf_op jit(solution)/shard_map/ppermute | solution.py:163
